TPU v7x, 32 devices: a whole 2x2x4 slice. The times are simulated.
32 devices in a mesh: pair: 8 (over z, x), row: 4 (over y, core).
Axes of the slice: x: 2, y: 2, z: 4, core: 2. Of those that a mesh axis runs over, the one named last changes fastest.
Arguments:
- records: bfloat16 [128, 4096, 8], P('row', 'pair'), may hold values from -10 to 10
- offsets: float32 [8, 128], P('pair', 'row'), may hold values from -1 to 1
- counts: int32 [8], replicated, may hold values from 64 to 128, as said below
- damping: float32 [1], replicated, may hold values from 0.1 to 1
Outputs:
- offset_step: float32 [8, 128], P('pair', 'row')
Inputs may be any that keep to these rules, and one draw needn't show every extreme that they name: Channel i of block b is live when i < counts[b]; in every draw some block has all 128 channels live.
All inputs are finite; a program needn't handle non-finite values.
Results may differ from a plain program's by a relative error of at most 0.0044.
Values may be sent and summed in bfloat16 or wider, within the bound.
No kernel may reach another device: no remote copies, remote signals or barrier semaphores. Data moves between devices by JAX's collectives and lax.ppermute only.
A program may use at most 64 MiB of HBM per device.

v0:
```python
import math
import jax
import jax.numpy as jnp
from jax import lax
from jax.sharding import PartitionSpec as P

CB = 128
NF = 512
NLAG = 256


def band_table(row_start, row_count, samples, first_bin, freq_count):
    sample_ids = row_start + jnp.arange(row_count, dtype=jnp.int32)
    freq_bins = first_bin + jnp.arange(freq_count, dtype=jnp.int32)
    phase_ids = sample_ids[:, None] * freq_bins[None, :] % samples
    angles = phase_ids.astype(jnp.float32) * (2.0 * math.pi / samples)
    return jnp.concatenate([jnp.cos(angles), jnp.sin(angles)], axis=1)


def lag_weights(samples, first_bin, freq_count, lag_count):
    freq_bins = first_bin + jnp.arange(freq_count, dtype=jnp.int32)
    lag_ids = 1 + jnp.arange(lag_count, dtype=jnp.int32)
    phase_ids = freq_bins[:, None] * lag_ids[None, :] % samples
    angles = phase_ids.astype(jnp.float32) * (2.0 * math.pi / samples)
    centre = (jnp.arange(freq_count, dtype=jnp.float32) + 0.5) * (math.pi / freq_count)
    weight = jnp.sin(centre) ** 2
    return (-2.0 * weight[:, None] * jnp.sin(angles)).astype(jnp.bfloat16)


def pair_stats(own_spec, partners, lag_table, angular):
    own_re = own_spec[:, 0].astype(jnp.float32)
    own_im = own_spec[:, 1].astype(jnp.float32)
    far_re = partners[:, :, 0].astype(jnp.float32)
    far_im = partners[:, :, 1].astype(jnp.float32)
    cross_re = own_re * far_re + own_im * far_im
    cross_im = own_im * far_re - own_re * far_im
    stacked = jnp.stack([cross_im, angular * cross_re]).astype(jnp.bfloat16)
    lagged = jnp.dot(stacked, lag_table, preferred_element_type=jnp.float32)
    residual = lagged[0]
    jacobian = lagged[1]
    return (jnp.sum(jacobian * jacobian, axis=-1), jnp.sum(jacobian * residual, axis=-1))


def per_device(records, offsets, counts, damping):
    nblock = lax.axis_size("pair")
    block_rank = lax.axis_index("pair")
    quarter = lax.axis_index("row")
    relaid = lax.all_to_all(records, "pair", split_axis=2, concat_axis=1, tiled=True)
    signal = relaid[:, :, 0]
    channels = signal.shape[0]
    samples = signal.shape[1]
    first_bin = samples // 8
    block_len = samples // 8

    def accumulate(partial_value, turn_index):
        first_row = turn_index * block_len
        segment = lax.dynamic_slice_in_dim(signal, first_row, block_len, 1)
        dft_table = band_table(first_row, block_len, samples, first_bin, NF)
        table_high = dft_table.astype(jnp.bfloat16)
        table_low = (dft_table - table_high.astype(jnp.float32)).astype(jnp.bfloat16)
        partial_value = partial_value + jnp.dot(
            segment, table_high, preferred_element_type=jnp.float32
        )
        partial_value = partial_value + jnp.dot(
            segment, table_low, preferred_element_type=jnp.float32
        )
        return (partial_value, None)

    spectrum, _ = lax.scan(
        accumulate, jnp.zeros((channels, 2 * NF), jnp.float32), jnp.arange(8, dtype=jnp.int32)
    )
    cosine_part = spectrum[:, :NF]
    sine_part = spectrum[:, NF:]
    angular = (first_bin + jnp.arange(NF, dtype=jnp.int32)).astype(jnp.float32) * (
        2.0 * math.pi / samples
    )
    shift_angle = offsets[0][:, None] * angular[None, :]
    shift_cos = jnp.cos(shift_angle)
    shift_sin = jnp.sin(shift_angle)
    real_part = cosine_part * shift_cos + sine_part * shift_sin
    imag_part = cosine_part * shift_sin - sine_part * shift_cos
    live_count = lax.dynamic_index_in_dim(counts, block_rank, keepdims=False)
    channel_ids = quarter * channels + jnp.arange(channels, dtype=jnp.int32)
    alive = (channel_ids < live_count).astype(jnp.float32)
    energy = jnp.mean(real_part * real_part + imag_part * imag_part, axis=1)
    weight_scale = alive / jnp.sqrt(energy + 1e-06)
    own_spec = jnp.stack(
        [real_part * weight_scale[:, None], imag_part * weight_scale[:, None]], axis=1
    ).astype(jnp.bfloat16)
    lag_table = lag_weights(samples, first_bin, NF, NLAG)
    segment = lax.all_gather(own_spec[None], "pair", axis=0, tiled=True)
    squares_part, products_part = pair_stats(own_spec, segment, lag_table, angular)
    partner_ids = jnp.arange(segment.shape[0], dtype=jnp.int32)
    keep_mask = (partner_ids > block_rank).astype(jnp.float32)[:, None]
    new_squares = squares_part * keep_mask
    new_products = products_part * keep_mask
    eye_blocks = jnp.eye(nblock, dtype=jnp.float32)
    onehot = (jnp.arange(nblock, dtype=jnp.int32) == block_rank).astype(jnp.float32)
    sq_t = new_squares.T
    pr_t = new_products.T
    crossing = sq_t[:, None, :] * onehot[None, :, None]
    diag_vals = sq_t + onehot[None, :] * jnp.sum(sq_t, axis=1, keepdims=True)
    hessian = diag_vals[:, :, None] * eye_blocks[None] - crossing - jnp.swapaxes(crossing, 1, 2)
    gradient = onehot[None, :] * jnp.sum(pr_t, axis=1, keepdims=True) - pr_t
    hessian, gradient = lax.psum((hessian, gradient), "pair")
    diagonal = jnp.diagonal(hessian, axis1=1, axis2=2)
    trace_sum = lax.psum(jnp.sum(diagonal), "row")
    level_mean = trace_sum / (nblock * CB)
    damped = damping[0] * (diagonal + level_mean)
    system = hessian + damped[:, :, None] * eye_blocks[None]
    factor = jnp.linalg.cholesky(system)
    update = -jax.scipy.linalg.cho_solve((factor, True), gradient[:, :, None])[:, :, 0]
    return lax.dynamic_slice_in_dim(update, block_rank, 1, 1).T


def solution(mesh):
    return jax.shard_map(
        per_device,
        mesh=mesh,
        in_specs=(P("row", "pair", None), P("pair", "row"), P(), P()),
        out_specs=P("pair", "row"),
        check_vma=False,
    )
```

profile of v0, /device:TPU:0, one launch (start us, length us, event | category | flops | bytes accessed | tf_op | source)
XLA Modules:
  0.0 172.0 jit_solution(3710374380044799579)
XLA Ops:
  0.0 1.7 %copy.35 = bf16[32,512,8]{1,0,2:T(8,128)(2,1)} copy(bf16[32,512,8]{1,2,0:T(8,128)(2,1)} %param.6) | data formatting | bytes 524288 | tf_op args[0]
  1.7 7.3 %all-to-all-start = ((bf16[32,512,8]{1,0,2:T(8,128)(2,1)}), bf16[32,512,8]{1,0,2:T(8,128)(2,1)S(1)}, u32[]{:S(2)}, u32[]{:S(2)}) async-start(bf16[32,512,8]{1,0,2:T(8,128)(2,1)} %copy.35), calls=%async_computation | async-start | bytes 524288 | tf_op jit(solution)/shard_map/all_to_all | solution.py:48
  9.2 0.6 dynamic_slice.20
  9.9 8.1 %all-to-all-done = bf16[32,512,8]{1,0,2:T(8,128)(2,1)S(1)} async-done(((bf16[32,512,8]{1,0,2:T(8,128)(2,1)}), bf16[32,512,8]{1,0,2:T(8,128)(2,1)S(1)}, u32[]{:S(2)}, u32[]{:S(2)}) %all-to-all-start) | async-done | bytes 262176 | tf_op jit(solution)/shard_map/all_to_all | solution.py:48
  18.0 48.9 %while.13 = (s32[]{:T(128)}, f32[32,1024]{1,0:T(8,128)S(1)}, s32[8]{0:T(128)S(1)}, bf16[32,4096]{1,0:T(8,128)(2,1)S(1)}, s32[]{:T(128)}, /*index=5*/s32[1]{0:T(128)}, s32[]{:T(128)}, s32[]{:T(128)}) while((s32[]{:T(128)}, f32[32,1024]{1,0:T(8,128)S(1)}, s32[8]{0:T(128)S(1)}, bf16[32,4096]{1,0:T(8,128)(2,1)S(1)}, s32[]{:T(128)}, ...), condition=%wide.region_1.2_spmd.clone, body=%wide.region_0.1_spmd.clone.sunk | while | flops 75596808 | bytes 6889645 | solution.py:69
  18.0 0.7 dynamic_slice.34
  19.4 4.1 %fusion.70 = (f32[512,512]{1,0:T(8,128)S(1)}, f32[512,512]{1,0:T(8,128)S(1)}) fusion(s32[512]{0:T(512)S(1)} %get-tuple-element.138, s32[512]{0:T(512)S(1)} %get-tuple-element.139), kind=kLoop, calls=%fused_computation.16.clone.1 | loop fusion | flops 3670016 | bytes 2101248 | tf_op jit(solution)/shard_map/while/body/eval_jaxpr/cos | solution.py:17
  24.1 0.7 dynamic_slice.34
  25.5 4.1 %fusion.70 = (f32[512,512]{1,0:T(8,128)S(1)}, f32[512,512]{1,0:T(8,128)S(1)}) fusion(s32[512]{0:T(512)S(1)} %get-tuple-element.138, s32[512]{0:T(512)S(1)} %get-tuple-element.139), kind=kLoop, calls=%fused_computation.16.clone.1 | loop fusion | flops 3670016 | bytes 2101248 | tf_op jit(solution)/shard_map/while/body/eval_jaxpr/cos | solution.py:17
  30.2 0.7 dynamic_slice.34
  31.6 4.1 %fusion.70 = (f32[512,512]{1,0:T(8,128)S(1)}, f32[512,512]{1,0:T(8,128)S(1)}) fusion(s32[512]{0:T(512)S(1)} %get-tuple-element.138, s32[512]{0:T(512)S(1)} %get-tuple-element.139), kind=kLoop, calls=%fused_computation.16.clone.1 | loop fusion | flops 3670016 | bytes 2101248 | tf_op jit(solution)/shard_map/while/body/eval_jaxpr/cos | solution.py:17
  36.3 0.7 dynamic_slice.34
  37.7 4.1 %fusion.70 = (f32[512,512]{1,0:T(8,128)S(1)}, f32[512,512]{1,0:T(8,128)S(1)}) fusion(s32[512]{0:T(512)S(1)} %get-tuple-element.138, s32[512]{0:T(512)S(1)} %get-tuple-element.139), kind=kLoop, calls=%fused_computation.16.clone.1 | loop fusion | flops 3670016 | bytes 2101248 | tf_op jit(solution)/shard_map/while/body/eval_jaxpr/cos | solution.py:17
  42.5 0.7 dynamic_slice.34
  43.8 4.1 %fusion.70 = (f32[512,512]{1,0:T(8,128)S(1)}, f32[512,512]{1,0:T(8,128)S(1)}) fusion(s32[512]{0:T(512)S(1)} %get-tuple-element.138, s32[512]{0:T(512)S(1)} %get-tuple-element.139), kind=kLoop, calls=%fused_computation.16.clone.1 | loop fusion | flops 3670016 | bytes 2101248 | tf_op jit(solution)/shard_map/while/body/eval_jaxpr/cos | solution.py:17
  48.6 0.7 dynamic_slice.34
  50.0 4.1 %fusion.70 = (f32[512,512]{1,0:T(8,128)S(1)}, f32[512,512]{1,0:T(8,128)S(1)}) fusion(s32[512]{0:T(512)S(1)} %get-tuple-element.138, s32[512]{0:T(512)S(1)} %get-tuple-element.139), kind=kLoop, calls=%fused_computation.16.clone.1 | loop fusion | flops 3670016 | bytes 2101248 | tf_op jit(solution)/shard_map/while/body/eval_jaxpr/cos | solution.py:17
  54.7 0.7 dynamic_slice.34
  56.1 4.1 %fusion.70 = (f32[512,512]{1,0:T(8,128)S(1)}, f32[512,512]{1,0:T(8,128)S(1)}) fusion(s32[512]{0:T(512)S(1)} %get-tuple-element.138, s32[512]{0:T(512)S(1)} %get-tuple-element.139), kind=kLoop, calls=%fused_computation.16.clone.1 | loop fusion | flops 3670016 | bytes 2101248 | tf_op jit(solution)/shard_map/while/body/eval_jaxpr/cos | solution.py:17
  60.8 0.7 dynamic_slice.34
  62.2 4.1 %fusion.70 = (f32[512,512]{1,0:T(8,128)S(1)}, f32[512,512]{1,0:T(8,128)S(1)}) fusion(s32[512]{0:T(512)S(1)} %get-tuple-element.138, s32[512]{0:T(512)S(1)} %get-tuple-element.139), kind=kLoop, calls=%fused_computation.16.clone.1 | loop fusion | flops 3670016 | bytes 2101248 | tf_op jit(solution)/shard_map/while/body/eval_jaxpr/cos | solution.py:17
  66.9 0.4 add_reduce_fusion
  67.4 0.6 compare_select_fusion
  68.1 31.6 %all_gather.3 = bf16[8,32,2,512]{3,1,0,2:T(8,128)(2,1)S(1)} all-gather(bf16[1,32,2,512]{3,1,0,2:T(8,128)(2,1)S(1)} %pad_maximum_fusion.1), channel_id=1, replica_groups=mesh['pair'=8,'row'=4] {'pair'}, dimensions={0}, use_global_device_ids=true | all-gather | bytes 589824 | tf_op jit(solution)/shard_map/all_gather | solution.py:91
  99.9 2.3 %fusion.28 = f32[2,8,32,256]{3,2,1,0:T(8,128)S(1)} fusion(bf16[1,8,32,512]{3,2,1,0:T(8,128)(2,1)S(1)} %get-tuple-element.99, bf16[1,8,32,512]{3,2,1,0:T(8,128)(2,1)S(1)} %get-tuple-element.98, s32[256]{0:T(256)S(1)} %iota_add_fusion.3, s32[512]{0:T(512)S(1)} %iota_add_fusion.2, f32[512]{0:T(512)S(1)} %multiply_multiply_fusion), kind=kOutput, calls=%fused_computation.45 | convolution fusion | flops 136577024 | bytes 1053696 | tf_op jit(solution)/shard_map/dot_general | solution.py:38
  102.6 35.2 %all-reduce = (f32[32,8,8]{0,1,2:T(8,128)S(1)}, f32[32,8]{0,1:T(8,128)S(1)}) all-reduce(f32[32,8,8]{0,1,2:T(8,128)S(1)} %multiply_subtract_fusion, f32[32,8]{0,1:T(8,128)S(1)} %get-tuple-element.104), channel_id=1, replica_groups=mesh['pair'=8,'row'=4] {'pair'}, use_global_device_ids=true, to_apply=%region_5.6 | all-reduce | flops 2304 | bytes 18432 | tf_op jit(solution)/shard_map/psum | solution.py:105
  137.8 0.6 gather_fusion
  138.4 0.7 reduce_sum.57
  139.7 6.3 %psum.22 = f32[]{:T(128)} all-reduce(f32[]{:T(128)} %reduce_sum.57), channel_id=1, replica_groups=mesh['pair'=8,'row'=4] {'row'}, use_global_device_ids=true, to_apply=%region_7.8 | all-reduce | flops 1 | bytes 8 | tf_op jit(solution)/shard_map/psum | solution.py:107
  146.9 23.5 %custom-call.11 = f32[32,8,8]{2,1,0:T(8,128)S(1)} custom-call(f32[32,8,8]{2,1,0:T(8,128)S(1)} %broadcast_multiply_fusion), custom_call_target="Cholesky" | custom-call | tf_op jit(solution)/shard_map/jit(cholesky)/cholesky | solution.py:111
  170.7 0.7 custom-call.12
  171.5 0.5 dynamic-slice_bitcast_fusion
  (61 shorter events, 6.1 us)
Async XLA Ops:
  0.0 9.2 %copy-start.1 = (s32[8]{0:T(128)S(1)}, s32[8]{0:T(128)}, u32[]{:S(2)}) copy-start(s32[8]{0:T(128)} %param.8) | copy-start | bytes 100
  1.7 16.2 %all-to-all-start = ((bf16[32,512,8]{1,0,2:T(8,128)(2,1)}), bf16[32,512,8]{1,0,2:T(8,128)(2,1)S(1)}, u32[]{:S(2)}, u32[]{:S(2)}) async-start(bf16[32,512,8]{1,0,2:T(8,128)(2,1)} %copy.35), calls=%async_computation | async-start | bytes 524288 | tf_op jit(solution)/shard_map/all_to_all | solution.py:48
  18.0 49.0 %copy-start = (f32[1,32]{1,0:T(1,128)S(1)}, f32[1,32]{1,0:T(1,128)}, u32[]{:S(2)}) copy-start(f32[1,32]{1,0:T(1,128)} %param.7) | copy-start | bytes 388
where the time goes:
time: 172 us
  blocking collectives  73.1 us (42%)
  other arithmetic  60.2 us (35%)
  local copies, waits for them, and re-layouts  9.21 us (5%)
  waiting for transfers between devices  8.06 us (5%)
  starting transfers between devices  7.28 us (4%)
  matrix products  6.83 us (4%)
  loops' own time  5.79 us (3%)
    psum x1, blocking collectives, per_device(): hessian, gradient = lax.psum((hessian, gradient), 'pair')  35.2 us
    cos x8, other arithmetic, band_table(): return jnp.concatenate([jnp.cos(angles), jnp.sin(angles)], axis=1)  33.2 us
    all_gather x1, blocking collectives, per_device(): segment = lax.all_gather(own_spec[None], 'pair', axis=0, tiled=True)  31.6 us
    another operation x4, other arithmetic, per_device(): factor = jnp.linalg.cholesky(system)  23.6 us
    all_to_all x1, waiting for transfers between devices, per_device(): lax.all_to_all(records, 'pair', split_axis=2, concat_axis=1, tiled=True)  8.06 us
    all_to_all x1, starting transfers between devices, per_device(): lax.all_to_all(records, 'pair', split_axis=2, concat_axis=1, tiled=True)  7.28 us
    psum x1, blocking collectives, per_device(): trace_sum = lax.psum(jnp.sum(diagonal), 'row')  6.25 us
    another operation x1, loops' own time, per_device(): lax.scan(accumulate, jnp.zeros((channels, 2 * NF), jnp.float32), jnp.aran...  5.79 us
  transfers between devices with their start and end apart: 1, of which 1 were waited for; matrix products, arithmetic and copies ran while one was open for 0% of the time, Pallas kernels for 0%

commit v1 on v0

--- a/solution.py
+++ b/solution.py
@@ -7,6 +7,24 @@
 CB = 128
 NF = 512
 NLAG = 256
+
+
+def in_order(tiles, dim):
+    tiles = jnp.moveaxis(tiles, 0, dim)
+    lengths = tiles.shape
+    return tiles.reshape(*lengths[:dim], lengths[dim] * lengths[dim + 1], *lengths[dim + 2 :])
+
+
+def collected_by_bits(shard, axis):
+    length = lax.axis_size(axis)
+    blocks = shard[None]
+    for level in range(length.bit_length() - 1):
+        bit = 1 << level
+        other = lax.ppermute(blocks, axis, [(i, i ^ bit) for i in range(length)])
+        both = jnp.stack([blocks, other])
+        upper = lax.axis_index(axis) >> level & 1
+        blocks = jnp.where(upper == 0, both, both[::-1]).reshape(-1, *shard.shape)
+    return blocks
 
 
 def band_table(row_start, row_count, samples, first_bin, freq_count):
@@ -88,7 +106,7 @@
         [real_part * weight_scale[:, None], imag_part * weight_scale[:, None]], axis=1
     ).astype(jnp.bfloat16)
     lag_table = lag_weights(samples, first_bin, NF, NLAG)
-    segment = lax.all_gather(own_spec[None], "pair", axis=0, tiled=True)
+    segment = in_order(collected_by_bits(own_spec[None], "pair"), 0)
     squares_part, products_part = pair_stats(own_spec, segment, lag_table, angular)
     partner_ids = jnp.arange(segment.shape[0], dtype=jnp.int32)
     keep_mask = (partner_ids > block_rank).astype(jnp.float32)[:, None]

time: 172 us -> 163 us (0.948)
  blocking collectives: 73.1 us -> 42.7 us
  waiting for transfers between devices: 8.06 us -> 24.2 us
  starting transfers between devices: 7.28 us -> 11.3 us
    all_gather x1 -> x0, blocking collectives: 31.6 us -> none  [per_device(): segment = lax.all_gather(own_spec[None], 'pair', axis=0, tiled=True)]
    ppermute x0 -> x3, waiting for transfers between devices: none -> 16 us  [collected_by_bits(): other = lax.ppermute(blocks, axis, [(i, i ^ bit) for i in range(length)])]
    ppermute x0 -> x3, starting transfers between devices: none -> 4.05 us  [collected_by_bits(): other = lax.ppermute(blocks, axis, [(i, i ^ bit) for i in range(length)])]
  transfers between devices with their start and end apart: 1 -> 4, of which waited for: 1 -> 4; matrix products, arithmetic and copies ran while one was open for 0% -> 0% of each run, Pallas kernels for 0% -> 0%
where the time goes in v1:
time: 163 us; the launch traced here: 162 us
  other arithmetic  60.7 us (37%)
  blocking collectives  42.7 us (26%)
  waiting for transfers between devices  24.2 us (15%)
  starting transfers between devices  11.3 us (7%)
  local copies, waits for them, and re-layouts  9.23 us (6%)
  matrix products  6.85 us (4%)
  loops' own time  5.79 us (4%)
    psum x1, blocking collectives, per_device(): hessian, gradient = lax.psum((hessian, gradient), 'pair')  36.5 us
    cos x8, other arithmetic, band_table(): return jnp.concatenate([jnp.cos(angles), jnp.sin(angles)], axis=1)  33.2 us
    another operation x4, other arithmetic, per_device(): factor = jnp.linalg.cholesky(system)  23.6 us
    ppermute x3, waiting for transfers between devices, collected_by_bits(): other = lax.ppermute(blocks, axis, [(i, i ^ bit) for i in range(length)])  16 us
    all_to_all x1, waiting for transfers between devices, per_device(): lax.all_to_all(records, 'pair', split_axis=2, concat_axis=1, tiled=True)  8.25 us
    all_to_all x1, starting transfers between devices, per_device(): lax.all_to_all(records, 'pair', split_axis=2, concat_axis=1, tiled=True)  7.28 us
    psum x1, blocking collectives, per_device(): trace_sum = lax.psum(jnp.sum(diagonal), 'row')  6.25 us
    another operation x1, loops' own time, per_device(): lax.scan(accumulate, jnp.zeros((channels, 2 * NF), jnp.float32), jnp.aran...  5.79 us
  transfers between devices with their start and end apart: 4, of which 4 were waited for; matrix products, arithmetic and copies ran while one was open for 0% of the time, Pallas kernels for 0%

profile of v1, /device:TPU:0, one launch (start us, length us, event | category | flops | bytes accessed | tf_op | source)
XLA Modules:
  0.0 162.4 jit_solution(14559352406243958486)
XLA Ops:
  0.0 1.7 %copy.38 = bf16[32,512,8]{1,0,2:T(8,128)(2,1)} copy(bf16[32,512,8]{1,2,0:T(8,128)(2,1)} %param.6) | data formatting | bytes 524288 | tf_op args[0]
  1.7 7.3 %all-to-all-start = ((bf16[32,512,8]{1,0,2:T(8,128)(2,1)}), bf16[32,512,8]{1,0,2:T(8,128)(2,1)S(1)}, u32[]{:S(2)}, u32[]{:S(2)}) async-start(bf16[32,512,8]{1,0,2:T(8,128)(2,1)} %copy.38), calls=%async_computation | async-start | bytes 524288 | tf_op jit(solution)/shard_map/all_to_all | solution.py:66
  9.7 8.2 %all-to-all-done = bf16[32,512,8]{1,0,2:T(8,128)(2,1)S(1)} async-done(((bf16[32,512,8]{1,0,2:T(8,128)(2,1)}), bf16[32,512,8]{1,0,2:T(8,128)(2,1)S(1)}, u32[]{:S(2)}, u32[]{:S(2)}) %all-to-all-start) | async-done | bytes 262176 | tf_op jit(solution)/shard_map/all_to_all | solution.py:66
  18.0 49.0 %while.13 = (s32[]{:T(128)}, f32[32,1024]{1,0:T(8,128)S(1)}, s32[8]{0:T(128)S(1)}, bf16[32,4096]{1,0:T(8,128)(2,1)S(1)}, s32[]{:T(128)}, /*index=5*/s32[1]{0:T(128)}, s32[]{:T(128)}, s32[]{:T(128)}) while((s32[]{:T(128)}, f32[32,1024]{1,0:T(8,128)S(1)}, s32[8]{0:T(128)S(1)}, bf16[32,4096]{1,0:T(8,128)(2,1)S(1)}, s32[]{:T(128)}, ...), condition=%wide.region_1.2_spmd.clone, body=%wide.region_0.1_spmd.clone.sunk | while | flops 75596808 | bytes 6889645 | solution.py:87
  18.0 0.7 dynamic_slice.34
  19.4 4.1 %fusion.69 = (f32[512,512]{1,0:T(8,128)S(1)}, f32[512,512]{1,0:T(8,128)S(1)}) fusion(s32[512]{0:T(512)S(1)} %get-tuple-element.137, s32[512]{0:T(512)S(1)} %get-tuple-element.138), kind=kLoop, calls=%fused_computation.16.clone.1 | loop fusion | flops 3670016 | bytes 2101248 | tf_op jit(solution)/shard_map/while/body/eval_jaxpr/cos | solution.py:35
  24.1 0.7 dynamic_slice.34
  25.5 4.1 %fusion.69 = (f32[512,512]{1,0:T(8,128)S(1)}, f32[512,512]{1,0:T(8,128)S(1)}) fusion(s32[512]{0:T(512)S(1)} %get-tuple-element.137, s32[512]{0:T(512)S(1)} %get-tuple-element.138), kind=kLoop, calls=%fused_computation.16.clone.1 | loop fusion | flops 3670016 | bytes 2101248 | tf_op jit(solution)/shard_map/while/body/eval_jaxpr/cos | solution.py:35
  30.2 0.7 dynamic_slice.34
  31.6 4.1 %fusion.69 = (f32[512,512]{1,0:T(8,128)S(1)}, f32[512,512]{1,0:T(8,128)S(1)}) fusion(s32[512]{0:T(512)S(1)} %get-tuple-element.137, s32[512]{0:T(512)S(1)} %get-tuple-element.138), kind=kLoop, calls=%fused_computation.16.clone.1 | loop fusion | flops 3670016 | bytes 2101248 | tf_op jit(solution)/shard_map/while/body/eval_jaxpr/cos | solution.py:35
  36.3 0.7 dynamic_slice.34
  37.7 4.1 %fusion.69 = (f32[512,512]{1,0:T(8,128)S(1)}, f32[512,512]{1,0:T(8,128)S(1)}) fusion(s32[512]{0:T(512)S(1)} %get-tuple-element.137, s32[512]{0:T(512)S(1)} %get-tuple-element.138), kind=kLoop, calls=%fused_computation.16.clone.1 | loop fusion | flops 3670016 | bytes 2101248 | tf_op jit(solution)/shard_map/while/body/eval_jaxpr/cos | solution.py:35
  42.5 0.7 dynamic_slice.34
  43.8 4.1 %fusion.69 = (f32[512,512]{1,0:T(8,128)S(1)}, f32[512,512]{1,0:T(8,128)S(1)}) fusion(s32[512]{0:T(512)S(1)} %get-tuple-element.137, s32[512]{0:T(512)S(1)} %get-tuple-element.138), kind=kLoop, calls=%fused_computation.16.clone.1 | loop fusion | flops 3670016 | bytes 2101248 | tf_op jit(solution)/shard_map/while/body/eval_jaxpr/cos | solution.py:35
  48.6 0.7 dynamic_slice.34
  50.0 4.1 %fusion.69 = (f32[512,512]{1,0:T(8,128)S(1)}, f32[512,512]{1,0:T(8,128)S(1)}) fusion(s32[512]{0:T(512)S(1)} %get-tuple-element.137, s32[512]{0:T(512)S(1)} %get-tuple-element.138), kind=kLoop, calls=%fused_computation.16.clone.1 | loop fusion | flops 3670016 | bytes 2101248 | tf_op jit(solution)/shard_map/while/body/eval_jaxpr/cos | solution.py:35
  54.7 0.7 dynamic_slice.34
  56.1 4.1 %fusion.69 = (f32[512,512]{1,0:T(8,128)S(1)}, f32[512,512]{1,0:T(8,128)S(1)}) fusion(s32[512]{0:T(512)S(1)} %get-tuple-element.137, s32[512]{0:T(512)S(1)} %get-tuple-element.138), kind=kLoop, calls=%fused_computation.16.clone.1 | loop fusion | flops 3670016 | bytes 2101248 | tf_op jit(solution)/shard_map/while/body/eval_jaxpr/cos | solution.py:35
  60.8 0.7 dynamic_slice.34
  62.2 4.1 %fusion.69 = (f32[512,512]{1,0:T(8,128)S(1)}, f32[512,512]{1,0:T(8,128)S(1)}) fusion(s32[512]{0:T(512)S(1)} %get-tuple-element.137, s32[512]{0:T(512)S(1)} %get-tuple-element.138), kind=kLoop, calls=%fused_computation.16.clone.1 | loop fusion | flops 3670016 | bytes 2101248 | tf_op jit(solution)/shard_map/while/body/eval_jaxpr/cos | solution.py:35
  68.4 1.5 collective-permute-start
  69.9 2.8 %collective-permute-done = bf16[1,1,32,2,512]{4,2,3,1,0:T(8,128)(2,1)S(1)} collective-permute-done((bf16[1,1,32,2,512]{4,2,3,1,0:T(8,128)(2,1)S(1)}, bf16[1,1,32,2,512]{4,2,3,1,0:T(8,128)(2,1)S(1)}, u32[]{:S(2)}, u32[]{:S(2)}) %collective-permute-start) | collective-permute-done | bytes 65568 | tf_op jit(solution)/shard_map/ppermute | solution.py:23
  72.8 1.1 collective-permute-start.1
  73.9 4.6 %collective-permute-done.1 = bf16[2,1,32,2,512]{4,2,3,0,1:T(8,128)(2,1)S(1)} collective-permute-done((bf16[2,1,32,2,512]{4,2,3,0,1:T(8,128)(2,1)S(1)}, bf16[2,1,32,2,512]{4,2,3,0,1:T(8,128)(2,1)S(1)}, u32[]{:S(2)}, u32[]{:S(2)}) %collective-permute-start.1) | collective-permute-done | bytes 131104 | tf_op jit(solution)/shard_map/ppermute | solution.py:23
  78.6 1.4 collective-permute-start.2
  80.1 8.6 %collective-permute-done.2 = bf16[4,1,32,2,512]{4,2,0,3,1:T(8,128)(2,1)S(1)} collective-permute-done((bf16[4,1,32,2,512]{4,2,0,3,1:T(8,128)(2,1)S(1)}, bf16[4,1,32,2,512]{4,2,0,3,1:T(8,128)(2,1)S(1)}, u32[]{:S(2)}, u32[]{:S(2)}) %collective-permute-start.2) | collective-permute-done | bytes 262176 | tf_op jit(solution)/shard_map/ppermute | solution.py:23
  89.1 2.3 %fusion.28 = f32[2,8,32,256]{3,2,1,0:T(8,128)S(1)} fusion(bf16[1,8,32,512]{3,2,1,0:T(8,128)(2,1)S(1)} %get-tuple-element.100, bf16[1,8,32,512]{3,2,1,0:T(8,128)(2,1)S(1)} %get-tuple-element.99, s32[256]{0:T(256)S(1)} %iota_add_fusion.3, s32[512]{0:T(512)S(1)} %iota_add_fusion.2, f32[512]{0:T(512)S(1)} %multiply_multiply_fusion), kind=kOutput, calls=%fused_computation.47 | convolution fusion | flops 136577024 | bytes 1053696 | tf_op jit(solution)/shard_map/dot_general | solution.py:56
  91.7 36.5 %all-reduce = (f32[32,8,8]{0,1,2:T(8,128)S(1)}, f32[32,8]{0,1:T(8,128)S(1)}) all-reduce(f32[32,8,8]{0,1,2:T(8,128)S(1)} %multiply_subtract_fusion, f32[32,8]{0,1:T(8,128)S(1)} %get-tuple-element.105), channel_id=1, replica_groups=mesh['pair'=8,'row'=4] {'pair'}, use_global_device_ids=true, to_apply=%region_5.6 | all-reduce | flops 2304 | bytes 18432 | tf_op jit(solution)/shard_map/psum | solution.py:123
  128.8 0.7 reduce_sum.57
  130.1 6.3 %psum.22 = f32[]{:T(128)} all-reduce(f32[]{:T(128)} %reduce_sum.57), channel_id=1, replica_groups=mesh['pair'=8,'row'=4] {'row'}, use_global_device_ids=true, to_apply=%region_7.8 | all-reduce | flops 1 | bytes 8 | tf_op jit(solution)/shard_map/psum | solution.py:125
  137.3 23.5 %custom-call.11 = f32[32,8,8]{2,1,0:T(8,128)S(1)} custom-call(f32[32,8,8]{2,1,0:T(8,128)S(1)} %broadcast_multiply_fusion), custom_call_target="Cholesky" | custom-call | tf_op jit(solution)/shard_map/jit(cholesky)/cholesky | solution.py:129
  161.1 0.7 custom-call.12
  (73 shorter events, 9.4 us)
Async XLA Ops:
  0.0 9.0 %copy-start.1 = (s32[8]{0:T(128)S(1)}, s32[8]{0:T(128)}, u32[]{:S(2)}) copy-start(s32[8]{0:T(128)} %param.8) | copy-start | bytes 100
  1.7 16.2 %all-to-all-start = ((bf16[32,512,8]{1,0,2:T(8,128)(2,1)}), bf16[32,512,8]{1,0,2:T(8,128)(2,1)S(1)}, u32[]{:S(2)}, u32[]{:S(2)}) async-start(bf16[32,512,8]{1,0,2:T(8,128)(2,1)} %copy.38), calls=%async_computation | async-start | bytes 524288 | tf_op jit(solution)/shard_map/all_to_all | solution.py:66
  18.0 49.0 %copy-start = (f32[1,32]{1,0:T(1,128)S(1)}, f32[1,32]{1,0:T(1,128)}, u32[]{:S(2)}) copy-start(f32[1,32]{1,0:T(1,128)} %param.7) | copy-start | bytes 388
  68.4 4.3 %collective-permute-start = (bf16[1,1,32,2,512]{4,2,3,1,0:T(8,128)(2,1)S(1)}, bf16[1,1,32,2,512]{4,2,3,1,0:T(8,128)(2,1)S(1)}, u32[]{:S(2)}, u32[]{:S(2)}) collective-permute-start(bf16[1,1,32,2,512]{4,2,3,1,0:T(8,128)(2,1)S(1)} %pad_maximum_fusion.4), channel_id=1, source_target_pairs={{0,4},{4,0},{8,12},{12,8},{16,20},{20,16},{24,28},{28,24},{1,5},{5... | collective-permute-start | bytes 196616 | tf_op jit(solution)/shard_map/ppermute | solution.py:23
  72.8 5.7 %collective-permute-start.1 = (bf16[2,1,32,2,512]{4,2,3,0,1:T(8,128)(2,1)S(1)}, bf16[2,1,32,2,512]{4,2,3,0,1:T(8,128)(2,1)S(1)}, u32[]{:S(2)}, u32[]{:S(2)}) collective-permute-start(bf16[2,1,32,2,512]{4,2,3,0,1:T(8,128)(2,1)S(1)} %get-tuple-element.104), channel_id=1, source_target_pairs={{0,8},{4,12},{8,0},{12,4},{16,24},{20,28},{24,16},{28,20},{1,9},{5... | collective-permute-start | bytes 393224 | tf_op jit(solution)/shard_map/ppermute | solution.py:23
  78.6 10.1 %collective-permute-start.2 = (bf16[4,1,32,2,512]{4,2,0,3,1:T(8,128)(2,1)S(1)}, bf16[4,1,32,2,512]{4,2,0,3,1:T(8,128)(2,1)S(1)}, u32[]{:S(2)}, u32[]{:S(2)}) collective-permute-start(bf16[4,1,32,2,512]{4,2,0,3,1:T(8,128)(2,1)S(1)} %copy.40), channel_id=1, source_target_pairs={{0,16},{4,20},{8,24},{12,28},{16,0},{20,4},{24,8},{28,12},{1,17},{... | collective-permute-start | bytes 786440 | tf_op jit(solution)/shard_map/ppermute | solution.py:23
